TPU v7x, 256 devices: a whole 4x4x8 slice. The times are simulated.
256 devices in a mesh: rows: 32 (over x, z_hi, core), cols: 8 (over z_lo, y).
Axes of the slice: x: 4, y: 4, z: 8 (z_hi: 4, z_lo: 2; z = z_hi * 2 + z_lo), core: 2. Of those that a mesh axis runs over, the one named last changes fastest.
Arguments:
- right_side: float32 [4, 8, 1024, 512], P(None, 'cols', 'rows'), may hold values from -6 to 6
- inverse_blocks: bfloat16 [4, 8, 1024, 8192], P(None, None, 'rows', 'cols'), may hold values from -0.09375 to 0.09375
- lower_blocks: bfloat16 [6, 8, 1024, 8192], P(None, None, 'rows', 'cols'), may hold values from -0.046875 to 0.046875
Outputs:
- solution: float32 [4, 8, 1024, 512], P(None, 'cols', 'rows')
All inputs are finite; a program needn't handle non-finite values.
Results may differ from a plain program's by a relative error of at most 0.014.
Values may be sent and summed in bfloat16 or wider, within the bound.
A program may use at most 64 MiB of HBM per device.

v0:
```python
import jax
import jax.numpy as jnp
from jax import lax
from jax.sharding import PartitionSpec as P


def pair_index(target, source):
    return target * (target - 1) // 2 + source


def product(factor_block, rows_all):
    return jnp.einsum("abk,kn->abn", factor_block, rows_all, preferred_element_type=jnp.float32)


def fold_rows(factor_block, incoming):
    return jnp.einsum("abk,kn->abn", factor_block, incoming[0], preferred_element_type=jnp.float32)


def forward_solve(right_side, inverse_blocks, lower_blocks):
    panels = right_side.shape[0]
    groups = inverse_blocks.shape[1]
    local_rows = inverse_blocks.shape[2]
    columns = right_side.shape[3]
    gathered = []
    solutions = []
    for current in range(panels):
        if current == 0:
            residual = right_side[0].astype(jnp.bfloat16)
        else:
            partial_value = jnp.zeros((groups, local_rows, columns), jnp.float32)
            for source in range(current):
                partial_value = partial_value + product(
                    lower_blocks[pair_index(current, source)], gathered[source]
                )
            shares = lax.psum_scatter(partial_value, "cols", scatter_dimension=0, tiled=True)
            residual = (right_side[current] - shares).astype(jnp.bfloat16)
        products = fold_rows(
            inverse_blocks[current], lax.all_gather(residual, "rows", axis=1, tiled=True)
        )
        solved = lax.psum_scatter(products, "cols", scatter_dimension=0, tiled=True)
        solutions.append(solved)
        if current + 1 < panels:
            rows_all = lax.all_gather(solved.astype(jnp.bfloat16), "rows", axis=1, tiled=True)[0]
            gathered.append(rows_all)
    return jnp.stack(solutions)


def body(right_side, inverse_blocks, lower_blocks):
    return forward_solve(right_side, inverse_blocks, lower_blocks)


def solution(mesh):
    return jax.shard_map(
        body,
        mesh=mesh,
        in_specs=(
            P(None, "cols", "rows", None),
            P(None, None, "rows", "cols"),
            P(None, None, "rows", "cols"),
        ),
        out_specs=P(None, "cols", "rows", None),
        check_vma=False,
    )
```

profile of v0, /device:TPU:2, one launch (start us, length us, event | category | flops | bytes accessed | tf_op | source)
XLA Modules:
  0.0 677.7 jit_solution(5792396489258277267)
XLA Ops:
  6.5 1.5 slice.102
  8.1 55.7 %all-gather.21.cloned.1.call-done = bf16[1,1,1024,512]{3,2,1,0:T(8,128)(2,1)} async-done(((bf16[1,1,32,512]{3,2,1,0:T(8,128)(2,1)}), bf16[1,1,1024,512]{3,2,1,0:T(8,128)(2,1)}) %all-gather.21.cloned.1.call-update) | async-done | bytes 1048592 | tf_op jit(solution)/shard_map/all_gather | solution.py:38
  63.8 2.6 fusion.2
  66.5 39.0 %reduce-scatter.8.cloned.1.call-done = f32[1,32,512]{2,1,0:T(8,128)} async-done(((f32[8,32,512]{2,1,0:T(8,128)}), f32[1,32,512]{2,1,0:T(8,128)}) %reduce-scatter.8.cloned.1.call-update) | async-done | bytes 65552 | tf_op jit(solution)/shard_map/reduce_scatter | solution.py:40
  105.5 1.5 convert_element_type.31
  107.0 51.0 %all-gather.9.cloned.1.call-done = bf16[1,1024,512]{2,1,0:T(8,128)(2,1)} async-done(((bf16[1,32,512]{2,1,0:T(8,128)(2,1)}), bf16[1,1024,512]{2,1,0:T(8,128)(2,1)}) %all-gather.9.cloned.1.call-update) | async-done | bytes 1048592 | tf_op jit(solution)/shard_map/all_gather | solution.py:43
  158.1 2.6 convolution_bitcast_fusion.3
  160.7 39.0 %reduce-scatter.10.cloned.1.call-done = f32[1,32,512]{2,1,0:T(8,128)} async-done(((f32[8,32,512]{2,1,0:T(8,128)}), f32[1,32,512]{2,1,0:T(8,128)}) %reduce-scatter.10.cloned.1.call-update) | async-done | bytes 65552 | tf_op jit(solution)/shard_map/reduce_scatter | solution.py:35
  199.8 1.5 fusion.37
  201.3 50.6 %all-gather.11.cloned.1.call-done = bf16[1,1024,512]{2,1,0:T(8,128)(2,1)} async-done(((bf16[1,32,512]{2,1,0:T(8,128)(2,1)}), bf16[1,1024,512]{2,1,0:T(8,128)(2,1)}) %all-gather.11.cloned.1.call-update) | async-done | bytes 1048592 | tf_op jit(solution)/shard_map/all_gather | solution.py:38
  251.9 2.5 convolution_bitcast_fusion.2
  254.4 39.0 %reduce-scatter.12.cloned.1.call-done = f32[1,32,512]{2,1,0:T(8,128)} async-done(((f32[8,32,512]{2,1,0:T(8,128)}), f32[1,32,512]{2,1,0:T(8,128)}) %reduce-scatter.12.cloned.1.call-update) | async-done | bytes 65552 | tf_op jit(solution)/shard_map/reduce_scatter | solution.py:40
  293.5 1.5 convert_element_type.33
  295.0 1.8 fusion.12
  296.8 49.2 %all-gather.13.cloned.1.call-done = bf16[1,1024,512]{2,1,0:T(8,128)(2,1)} async-done(((bf16[1,32,512]{2,1,0:T(8,128)(2,1)}), bf16[1,1024,512]{2,1,0:T(8,128)(2,1)}) %all-gather.13.cloned.1.call-update) | async-done | bytes 1048592 | tf_op jit(solution)/shard_map/all_gather | solution.py:43
  346.0 2.6 fusion.1
  348.7 39.1 %reduce-scatter.14.cloned.1.call-done = f32[1,32,512]{2,1,0:T(8,128)} async-done(((f32[8,32,512]{2,1,0:T(8,128)}), f32[1,32,512]{2,1,0:T(8,128)}) %reduce-scatter.14.cloned.1.call-update) | async-done | bytes 65552 | tf_op jit(solution)/shard_map/reduce_scatter | solution.py:35
  387.7 1.5 fusion.36
  389.3 50.7 %all-gather.15.cloned.1.call-done = bf16[1,1024,512]{2,1,0:T(8,128)(2,1)} async-done(((bf16[1,32,512]{2,1,0:T(8,128)(2,1)}), bf16[1,1024,512]{2,1,0:T(8,128)(2,1)}) %all-gather.15.cloned.1.call-update) | async-done | bytes 1048592 | tf_op jit(solution)/shard_map/all_gather | solution.py:38
  439.9 2.5 convolution_bitcast_fusion.1
  442.5 39.0 %reduce-scatter.16.cloned.1.call-done = f32[1,32,512]{2,1,0:T(8,128)} async-done(((f32[8,32,512]{2,1,0:T(8,128)}), f32[1,32,512]{2,1,0:T(8,128)}) %reduce-scatter.16.cloned.1.call-update) | async-done | bytes 65552 | tf_op jit(solution)/shard_map/reduce_scatter | solution.py:40
  481.5 1.5 convert_element_type.35
  483.0 1.8 fusion.10
  484.8 1.8 convolution_add_fusion.1
  486.6 47.4 %all-gather.17.cloned.1.call-done = bf16[1,1024,512]{2,1,0:T(8,128)(2,1)} async-done(((bf16[1,32,512]{2,1,0:T(8,128)(2,1)}), bf16[1,1024,512]{2,1,0:T(8,128)(2,1)}) %all-gather.17.cloned.1.call-update) | async-done | bytes 1048592 | tf_op jit(solution)/shard_map/all_gather | solution.py:43
  534.0 2.6 fusion
  536.7 39.0 %reduce-scatter.18.cloned.1.call-done = f32[1,32,512]{2,1,0:T(8,128)} async-done(((f32[8,32,512]{2,1,0:T(8,128)}), f32[1,32,512]{2,1,0:T(8,128)}) %reduce-scatter.18.cloned.1.call-update) | async-done | bytes 65552 | tf_op jit(solution)/shard_map/reduce_scatter | solution.py:35
  575.7 1.5 fusion.35
  577.2 50.7 %all-gather.19.cloned.1.call-done = bf16[1,1024,512]{2,1,0:T(8,128)(2,1)} async-done(((bf16[1,32,512]{2,1,0:T(8,128)(2,1)}), bf16[1,1024,512]{2,1,0:T(8,128)(2,1)}) %all-gather.19.cloned.1.call-update) | async-done | bytes 1048592 | tf_op jit(solution)/shard_map/all_gather | solution.py:38
  628.0 2.5 convolution_bitcast_fusion
  630.5 39.1 %reduce-scatter.20.cloned.1.call-done = f32[1,32,512]{2,1,0:T(8,128)} async-done(((f32[8,32,512]{2,1,0:T(8,128)}), f32[1,32,512]{2,1,0:T(8,128)}) %reduce-scatter.20.cloned.1.call-update) | async-done | bytes 65552 | tf_op jit(solution)/shard_map/reduce_scatter | solution.py:40
  669.6 1.6 pad_maximum_fusion
  (38 shorter events, 0.8 us)
Async XLA Ops:
  6.5 57.2 %all-gather.21.cloned.1.call-start = ((), (), s32[]{:S(2)}) async-start(), calls=%async_computation.20 | async-start | bytes 1081344 | tf_op jit(solution)/shard_map/all_gather | solution.py:38
  8.0 191.7 %copy-start.3 = (f32[4,1,32,512]{3,2,1,0:T(8,128)S(1)}, f32[4,1,32,512]{3,2,1,0:T(8,128)}, u32[]{:S(2)}) copy-start(f32[4,1,32,512]{3,2,1,0:T(8,128)} %param.3) | copy-start | bytes 786436
  8.0 97.5 %reduce-scatter.8.cloned.1.call-start = ((), (), s32[]{:S(2)}) async-start(), calls=%async_computation.7 | async-start | bytes 589824 | tf_op jit(solution)/shard_map/reduce_scatter | solution.py:40
  66.4 185.5 %copy-start.4 = (bf16[4,8,32,1024]{3,2,1,0:T(8,128)(2,1)S(1)}, bf16[4,8,32,1024]{3,2,1,0:T(8,128)(2,1)}, u32[]{:S(2)}) copy-start(bf16[4,8,32,1024]{3,2,1,0:T(8,128)(2,1)} %param.4) | copy-start | bytes 6291460
  66.4 91.6 %all-gather.9.cloned.1.call-start = ((), (), s32[]{:S(2)}) async-start(), calls=%async_computation.8 | async-start | bytes 1081344 | tf_op jit(solution)/shard_map/all_gather | solution.py:43
  107.0 92.8 %reduce-scatter.10.cloned.1.call-start = ((), (), s32[]{:S(2)}) async-start(), calls=%async_computation.9 | async-start | bytes 589824 | tf_op jit(solution)/shard_map/reduce_scatter | solution.py:35
  160.7 91.2 %all-gather.11.cloned.1.call-start = ((), (), s32[]{:S(2)}) async-start(), calls=%async_computation.10 | async-start | bytes 1081344 | tf_op jit(solution)/shard_map/all_gather | solution.py:38
  201.2 92.2 %reduce-scatter.12.cloned.1.call-start = ((), (), s32[]{:S(2)}) async-start(), calls=%async_computation.11 | async-start | bytes 589824 | tf_op jit(solution)/shard_map/reduce_scatter | solution.py:40
  254.4 91.6 %all-gather.13.cloned.1.call-start = ((), (), s32[]{:S(2)}) async-start(), calls=%async_computation.12 | async-start | bytes 1081344 | tf_op jit(solution)/shard_map/all_gather | solution.py:43
  295.0 92.8 %reduce-scatter.14.cloned.1.call-start = ((), (), s32[]{:S(2)}) async-start(), calls=%async_computation.13 | async-start | bytes 589824 | tf_op jit(solution)/shard_map/reduce_scatter | solution.py:35
  348.6 91.3 %all-gather.15.cloned.1.call-start = ((), (), s32[]{:S(2)}) async-start(), calls=%async_computation.14 | async-start | bytes 1081344 | tf_op jit(solution)/shard_map/all_gather | solution.py:38
  389.2 92.3 %reduce-scatter.16.cloned.1.call-start = ((), (), s32[]{:S(2)}) async-start(), calls=%async_computation.15 | async-start | bytes 589824 | tf_op jit(solution)/shard_map/reduce_scatter | solution.py:40
  442.4 91.6 %all-gather.17.cloned.1.call-start = ((), (), s32[]{:S(2)}) async-start(), calls=%async_computation.16 | async-start | bytes 1081344 | tf_op jit(solution)/shard_map/all_gather | solution.py:43
  483.0 92.8 %reduce-scatter.18.cloned.1.call-start = ((), (), s32[]{:S(2)}) async-start(), calls=%async_computation.17 | async-start | bytes 589824 | tf_op jit(solution)/shard_map/reduce_scatter | solution.py:35
  536.6 132.9 %copy-start = (f32[1,32,512]{2,1,0:T(8,128)S(1)}, f32[1,32,512]{2,1,0:T(8,128)}, u32[]{:S(2)}) copy-start(f32[1,32,512]{2,1,0:T(8,128)} %reduce-scatter.8.cloned.1.call-done) | copy-start | bytes 196612
  536.6 132.9 %copy-start.1 = (f32[1,32,512]{2,1,0:T(8,128)S(1)}, f32[1,32,512]{2,1,0:T(8,128)}, u32[]{:S(2)}) copy-start(f32[1,32,512]{2,1,0:T(8,128)} %reduce-scatter.12.cloned.1.call-done) | copy-start | bytes 196612
  536.6 132.9 %copy-start.2 = (f32[1,32,512]{2,1,0:T(8,128)S(1)}, f32[1,32,512]{2,1,0:T(8,128)}, u32[]{:S(2)}) copy-start(f32[1,32,512]{2,1,0:T(8,128)} %reduce-scatter.16.cloned.1.call-done) | copy-start | bytes 196612
  536.7 91.3 %all-gather.19.cloned.1.call-start = ((), (), s32[]{:S(2)}) async-start(), calls=%async_computation.18 | async-start | bytes 1081344 | tf_op jit(solution)/shard_map/all_gather | solution.py:38
  577.2 92.4 %reduce-scatter.20.cloned.1.call-start = ((), (), s32[]{:S(2)}) async-start(), calls=%async_computation.19 | async-start | bytes 589824 | tf_op jit(solution)/shard_map/reduce_scatter | solution.py:40
Sparse Core Ops, SparseCore 0:
  9.9 53.8 all-gather.20
  66.6 38.8 reduce-scatter.7
  108.4 49.6 all-gather.8
  160.8 38.8 reduce-scatter.9
  202.2 49.6 all-gather.10
  254.5 38.9 reduce-scatter.11
  296.3 49.5 all-gather.12
  348.7 38.9 reduce-scatter.13
  390.3 49.5 all-gather.14
  442.5 38.8 reduce-scatter.15
  484.4 49.6 all-gather.16
  536.8 38.8 reduce-scatter.17
  578.3 49.6 all-gather.18
  630.6 38.9 reduce-scatter.19
where the time goes:
time: 678 us
  waiting for transfers between devices  629 us (93%)
  matrix products  23.2 us (3%)
  between operations  13.3 us (2%)
  other arithmetic  10.3 us (2%)
    all_gather x4, waiting for transfers between devices, forward_solve(): lax.all_gather(residual, 'rows', axis=1, tiled=True)  208 us
    reduce_scatter x4, waiting for transfers between devices, forward_solve(): solved = lax.psum_scatter(products, 'cols', scatter_dimension=0, tiled=True)  156 us
    all_gather x3, waiting for transfers between devices, forward_solve(): lax.all_gather(solved.astype(jnp.bfloat16), 'rows', axis=1, tiled=True)[0]  148 us
    reduce_scatter x3, waiting for transfers between devices, forward_solve(): lax.psum_scatter(partial_value, 'cols', scatter_dimension=0, tiled=True)  117 us
  transfers between devices with their start and end apart: 14, of which 14 were waited for; matrix products, arithmetic and copies ran while one was open for 1% of the time, Pallas kernels for 0%

commit v1 on v0

--- a/solution.py
+++ b/solution.py
@@ -2,6 +2,15 @@
 import jax.numpy as jnp
 from jax import lax
 from jax.sharding import PartitionSpec as P
+
+
+def read_plate(piece_in, device_axis):
+    return jnp.concatenate(
+        lax.all_to_all(
+            jnp.stack([piece_in for _ in range(lax.psum(1, device_axis))], 0), device_axis, 0, 0
+        ),
+        1,
+    )
 
 
 def pair_index(target, source):
@@ -34,9 +43,7 @@
                 )
             shares = lax.psum_scatter(partial_value, "cols", scatter_dimension=0, tiled=True)
             residual = (right_side[current] - shares).astype(jnp.bfloat16)
-        products = fold_rows(
-            inverse_blocks[current], lax.all_gather(residual, "rows", axis=1, tiled=True)
-        )
+        products = fold_rows(inverse_blocks[current], read_plate(residual, device_axis="rows"))
         solved = lax.psum_scatter(products, "cols", scatter_dimension=0, tiled=True)
         solutions.append(solved)
         if current + 1 < panels:

time: 678 us -> 606 us (0.89)
  waiting for transfers between devices: 629 us -> 424 us
  blocking collectives: 0 us -> 139 us
    all_gather x4 -> x0, waiting for transfers between devices: 208 us -> none  [forward_solve(): lax.all_gather(residual, 'rows', axis=1, tiled=True)]
    all_to_all x0 -> x4, blocking collectives: none -> 139 us  [read_plate(): lax.all_to_all(jnp.stack([piece_in for _ in range(lax.psum(1, device_axis...]
  transfers between devices with their start and end apart: 14 -> 10, of which waited for: 14 -> 10; matrix products, arithmetic and copies ran while one was open for 1% -> 1% of each run, Pallas kernels for 0% -> 0%
where the time goes in v1:
time: 606 us; the launch traced here: 605 us
  waiting for transfers between devices  424 us (70%)
  blocking collectives  139 us (23%)
  matrix products  18.3 us (3%)
  between operations  13.7 us (2%)
  other arithmetic  8.49 us (1%)
    reduce_scatter x4, waiting for transfers between devices, forward_solve(): solved = lax.psum_scatter(products, 'cols', scatter_dimension=0, tiled=True)  159 us
    all_gather x3, waiting for transfers between devices, forward_solve(): lax.all_gather(solved.astype(jnp.bfloat16), 'rows', axis=1, tiled=True)[0]  148 us
    all_to_all x4, blocking collectives, read_plate(): lax.all_to_all(jnp.stack([piece_in for _ in range(lax.psum(1, device_axis...  139 us
    reduce_scatter x3, waiting for transfers between devices, forward_solve(): lax.psum_scatter(partial_value, 'cols', scatter_dimension=0, tiled=True)  117 us
    dot_general x6, matrix products, product(): jnp.einsum('abk,kn->abn', factor_block, rows_all, preferred_element_type=...  13.3 us
  transfers between devices with their start and end apart: 10, of which 10 were waited for; matrix products, arithmetic and copies ran while one was open for 1% of the time, Pallas kernels for 0%

profile of v1, /device:TPU:2, one launch (start us, length us, event | category | flops | bytes accessed | tf_op | source)
XLA Modules:
  0.0 605.1 jit_solution(910487825803751694)
XLA Ops:
  6.5 1.0 fusion.37
  7.7 39.1 %all_to_all.20 = bf16[32,1,32,512]{3,2,1,0:T(8,128)(2,1)S(1)} all-to-all(bf16[32,1,32,512]{3,2,1,0:T(8,128)(2,1)S(1)} %stack.21), channel_id=1, replica_groups=mesh['rows'=32,'cols'=8] {'rows'}, dimensions={0} | all-to-all | bytes 2097152 | tf_op jit(solution)/shard_map/all_to_all | solution.py:9
  46.7 1.3 fusion.19
  48.1 38.2 %reduce-scatter.8.cloned.1.call-done = f32[1,32,512]{2,1,0:T(8,128)} async-done(((f32[8,32,512]{2,1,0:T(8,128)}), f32[1,32,512]{2,1,0:T(8,128)}) %reduce-scatter.8.cloned.1.call-update) | async-done | bytes 65552 | tf_op jit(solution)/shard_map/reduce_scatter | solution.py:47
  86.3 1.5 convert_element_type.28
  87.8 51.0 %all-gather.4.cloned.1.call-done = bf16[1,1024,512]{2,1,0:T(8,128)(2,1)} async-done(((bf16[1,32,512]{2,1,0:T(8,128)(2,1)}), bf16[1,1024,512]{2,1,0:T(8,128)(2,1)}) %all-gather.4.cloned.1.call-update) | async-done | bytes 1048592 | tf_op jit(solution)/shard_map/all_gather | solution.py:50
  138.8 2.6 convolution_bitcast_fusion.3
  141.5 39.0 %reduce-scatter.10.cloned.1.call-done = f32[1,32,512]{2,1,0:T(8,128)} async-done(((f32[8,32,512]{2,1,0:T(8,128)}), f32[1,32,512]{2,1,0:T(8,128)}) %reduce-scatter.10.cloned.1.call-update) | async-done | bytes 65552 | tf_op jit(solution)/shard_map/reduce_scatter | solution.py:44
  180.5 0.9 fusion.34
  181.5 33.3 %all_to_all.21 = bf16[32,1,32,512]{3,2,1,0:T(8,128)(2,1)S(1)} all-to-all(bf16[32,1,32,512]{3,2,1,0:T(8,128)(2,1)S(1)} %stack.23), channel_id=1, replica_groups=mesh['rows'=32,'cols'=8] {'rows'}, dimensions={0} | all-to-all | bytes 2097152 | tf_op jit(solution)/shard_map/all_to_all | solution.py:9
  214.8 1.2 convolution_bitcast_fusion.2
  216.1 40.3 %reduce-scatter.12.cloned.1.call-done = f32[1,32,512]{2,1,0:T(8,128)} async-done(((f32[8,32,512]{2,1,0:T(8,128)}), f32[1,32,512]{2,1,0:T(8,128)}) %reduce-scatter.12.cloned.1.call-update) | async-done | bytes 65552 | tf_op jit(solution)/shard_map/reduce_scatter | solution.py:47
  256.4 1.5 convert_element_type.31
  257.9 2.3 fusion.7
  260.2 48.6 %all-gather.6.cloned.1.call-done = bf16[1,1024,512]{2,1,0:T(8,128)(2,1)} async-done(((bf16[1,32,512]{2,1,0:T(8,128)(2,1)}), bf16[1,1024,512]{2,1,0:T(8,128)(2,1)}) %all-gather.6.cloned.1.call-update) | async-done | bytes 1048592 | tf_op jit(solution)/shard_map/all_gather | solution.py:50
  308.8 2.8 fusion.1
  311.7 39.1 %reduce-scatter.14.cloned.1.call-done = f32[1,32,512]{2,1,0:T(8,128)} async-done(((f32[8,32,512]{2,1,0:T(8,128)}), f32[1,32,512]{2,1,0:T(8,128)}) %reduce-scatter.14.cloned.1.call-update) | async-done | bytes 65552 | tf_op jit(solution)/shard_map/reduce_scatter | solution.py:44
  350.7 0.8 fusion.35
  351.7 33.5 %all_to_all.22 = bf16[32,1,32,512]{3,2,1,0:T(8,128)(2,1)S(1)} all-to-all(bf16[32,1,32,512]{3,2,1,0:T(8,128)(2,1)S(1)} %stack.25), channel_id=1, replica_groups=mesh['rows'=32,'cols'=8] {'rows'}, dimensions={0} | all-to-all | bytes 2097152 | tf_op jit(solution)/shard_map/all_to_all | solution.py:9
  385.2 1.3 convolution_bitcast_fusion.1
  386.5 40.0 %reduce-scatter.16.cloned.1.call-done = f32[1,32,512]{2,1,0:T(8,128)} async-done(((f32[8,32,512]{2,1,0:T(8,128)}), f32[1,32,512]{2,1,0:T(8,128)}) %reduce-scatter.16.cloned.1.call-update) | async-done | bytes 65552 | tf_op jit(solution)/shard_map/reduce_scatter | solution.py:47
  426.5 1.5 convert_element_type.34
  428.0 1.6 fusion.5
  429.6 1.5 convolution_add_fusion.1
  431.1 48.0 %all-gather.8.cloned.1.call-done = bf16[1,1024,512]{2,1,0:T(8,128)(2,1)} async-done(((bf16[1,32,512]{2,1,0:T(8,128)(2,1)}), bf16[1,1024,512]{2,1,0:T(8,128)(2,1)}) %all-gather.8.cloned.1.call-update) | async-done | bytes 1048592 | tf_op jit(solution)/shard_map/all_gather | solution.py:50
  479.0 2.6 fusion
  481.7 39.0 %reduce-scatter.18.cloned.1.call-done = f32[1,32,512]{2,1,0:T(8,128)} async-done(((f32[8,32,512]{2,1,0:T(8,128)}), f32[1,32,512]{2,1,0:T(8,128)}) %reduce-scatter.18.cloned.1.call-update) | async-done | bytes 65552 | tf_op jit(solution)/shard_map/reduce_scatter | solution.py:44
  520.7 0.8 fusion.36
  521.7 33.3 %all_to_all.23 = bf16[32,1,32,512]{3,2,1,0:T(8,128)(2,1)S(1)} all-to-all(bf16[32,1,32,512]{3,2,1,0:T(8,128)(2,1)S(1)} %stack.27), channel_id=1, replica_groups=mesh['rows'=32,'cols'=8] {'rows'}, dimensions={0} | all-to-all | bytes 2097152 | tf_op jit(solution)/shard_map/all_to_all | solution.py:9
  555.1 1.2 convolution_bitcast_fusion
  556.3 40.4 %reduce-scatter.20.cloned.1.call-done = f32[1,32,512]{2,1,0:T(8,128)} async-done(((f32[8,32,512]{2,1,0:T(8,128)}), f32[1,32,512]{2,1,0:T(8,128)}) %reduce-scatter.20.cloned.1.call-update) | async-done | bytes 65552 | tf_op jit(solution)/shard_map/reduce_scatter | solution.py:47
  596.7 1.6 pad_maximum_fusion
  (38 shorter events, 1.0 us)
Async XLA Ops:
  6.5 40.2 %copy-start.4 = (bf16[4,8,32,1024]{3,2,1,0:T(8,128)(2,1)S(1)}, bf16[4,8,32,1024]{3,2,1,0:T(8,128)(2,1)}, u32[]{:S(2)}) copy-start(bf16[4,8,32,1024]{3,2,1,0:T(8,128)(2,1)} %param.4) | copy-start | bytes 6291460
  6.5 79.8 %reduce-scatter.8.cloned.1.call-start = ((), (), s32[]{:S(2)}) async-start(), calls=%async_computation.11 | async-start | bytes 589824 | tf_op jit(solution)/shard_map/reduce_scatter | solution.py:47
  46.7 133.7 %copy-start.3 = (f32[4,1,32,512]{3,2,1,0:T(8,128)S(1)}, f32[4,1,32,512]{3,2,1,0:T(8,128)}, u32[]{:S(2)}) copy-start(f32[4,1,32,512]{3,2,1,0:T(8,128)} %param.3) | copy-start | bytes 786436
  48.0 90.8 %all-gather.4.cloned.1.call-start = ((), (), s32[]{:S(2)}) async-start(), calls=%async_computation.12 | async-start | bytes 1081344 | tf_op jit(solution)/shard_map/all_gather | solution.py:50
  87.8 92.7 %reduce-scatter.10.cloned.1.call-start = ((), (), s32[]{:S(2)}) async-start(), calls=%async_computation.13 | async-start | bytes 589824 | tf_op jit(solution)/shard_map/reduce_scatter | solution.py:44
  141.4 115.0 %reduce-scatter.12.cloned.1.call-start = ((), (), s32[]{:S(2)}) async-start(), calls=%async_computation.14 | async-start | bytes 589824 | tf_op jit(solution)/shard_map/reduce_scatter | solution.py:47
  181.5 76.5 %copy-start.5 = (bf16[1,1024,512]{2,1,0:T(8,128)(2,1)S(1)}, bf16[1,1024,512]{2,1,0:T(8,128)(2,1)}, u32[]{:S(2)}) copy-start(bf16[1,1024,512]{2,1,0:T(8,128)(2,1)} %all-gather.4.cloned.1.call-done) | copy-start | bytes 3145732
  216.0 92.8 %all-gather.6.cloned.1.call-start = ((), (), s32[]{:S(2)}) async-start(), calls=%async_computation.15 | async-start | bytes 1081344 | tf_op jit(solution)/shard_map/all_gather | solution.py:50
  257.9 92.8 %reduce-scatter.14.cloned.1.call-start = ((), (), s32[]{:S(2)}) async-start(), calls=%async_computation.16 | async-start | bytes 589824 | tf_op jit(solution)/shard_map/reduce_scatter | solution.py:44
  311.6 114.9 %reduce-scatter.16.cloned.1.call-start = ((), (), s32[]{:S(2)}) async-start(), calls=%async_computation.17 | async-start | bytes 589824 | tf_op jit(solution)/shard_map/reduce_scatter | solution.py:47
  386.4 92.6 %all-gather.8.cloned.1.call-start = ((), (), s32[]{:S(2)}) async-start(), calls=%async_computation.18 | async-start | bytes 1081344 | tf_op jit(solution)/shard_map/all_gather | solution.py:50
  428.0 92.8 %reduce-scatter.18.cloned.1.call-start = ((), (), s32[]{:S(2)}) async-start(), calls=%async_computation.19 | async-start | bytes 589824 | tf_op jit(solution)/shard_map/reduce_scatter | solution.py:44
  428.0 1.6 copy-start.6
  481.7 115.0 %reduce-scatter.20.cloned.1.call-start = ((), (), s32[]{:S(2)}) async-start(), calls=%async_computation.20 | async-start | bytes 589824 | tf_op jit(solution)/shard_map/reduce_scatter | solution.py:47
  521.7 75.0 %copy-start = (f32[1,32,512]{2,1,0:T(8,128)S(1)}, f32[1,32,512]{2,1,0:T(8,128)}, u32[]{:S(2)}) copy-start(f32[1,32,512]{2,1,0:T(8,128)} %reduce-scatter.8.cloned.1.call-done) | copy-start | bytes 196612
  521.7 75.0 %copy-start.1 = (f32[1,32,512]{2,1,0:T(8,128)S(1)}, f32[1,32,512]{2,1,0:T(8,128)}, u32[]{:S(2)}) copy-start(f32[1,32,512]{2,1,0:T(8,128)} %reduce-scatter.12.cloned.1.call-done) | copy-start | bytes 196612
  521.7 75.0 %copy-start.2 = (f32[1,32,512]{2,1,0:T(8,128)S(1)}, f32[1,32,512]{2,1,0:T(8,128)}, u32[]{:S(2)}) copy-start(f32[1,32,512]{2,1,0:T(8,128)} %reduce-scatter.16.cloned.1.call-done) | copy-start | bytes 196612
Sparse Core Ops, SparseCore 0:
  48.1 38.1 reduce-scatter.7
  89.2 49.6 all-gather.3
  141.6 38.8 reduce-scatter.9
  216.2 40.1 reduce-scatter.11
  259.1 49.6 all-gather.5
  311.7 38.9 reduce-scatter.13
  386.6 39.8 reduce-scatter.15
  429.4 49.6 all-gather.7
  481.8 38.9 reduce-scatter.17
  556.5 40.1 reduce-scatter.19
